TPU v7x, 32 devices: a whole 2x2x4 slice. The times are simulated.
32 devices in a mesh: groups: 2 (over x), row: 16 (over z, y, core).
Axes of the slice: x: 2, y: 2, z: 4, core: 2. Of those that a mesh axis runs over, the one named last changes fastest.
Arguments:
- inverse: float32 [4, 4096, 4096], P('groups', 'row'), parts along dimension 0, as said below
- cycle: bfloat16 [4, 4096, 1024], P('groups', 'row'), parts along dimension 0, as said below
- arrivals: bfloat16 [4, 2, 4096, 128], P('groups', None, 'row'), parts along dimension 0, may hold values from -6 to 6
- departing: int32 [4, 128], P('groups'), parts along dimension 0, may hold values from 0 to 1023, as said below
- directions: int32 [4, 512], P('groups'), parts along dimension 0, may hold values from 0 to 8191
Outputs:
- new_inverse: float32 [4, 4096, 4096], P('groups', 'row'), parts along dimension 0
- beam_weights: float32 [4, 2, 4096, 512], P('groups', None, 'row'), parts along dimension 0
- spectrum: float32 [4, 512], P('groups'), parts along dimension 0
There are 2 independent parts, one for each index of `groups`. A program takes and returns all parts, laid end to end along the dimension named above; each array names one. Nothing has to cross between parts.
Inputs may be any that keep to these rules, and one draw needn't show every extreme that they name: inverse is Hermitian and is the inverse of I + cycle cycle^H / 1024. `cycle`: the snapshots whose inverse covariance is given. `departing`: all 2 x 128 entries are different slots.
All inputs are finite; a program needn't handle non-finite values.
Results may differ from a plain program's by a relative error of at most 0.0003.
Values may be sent and summed in bfloat16 or wider, within the bound.
No kernel may reach another device: no remote copies, remote signals or barrier semaphores. Data moves between devices by JAX's collectives and lax.ppermute only.
A program may use at most 192 MiB of HBM per device.

v0:
```python
import jax
import jax.numpy as jnp
from jax import lax
from jax.sharding import PartitionSpec as P

M = 4096
CYCLE = 1024
STEPS = 2
precise = lax.Precision.HIGHEST


def matmul(left, right):
    return jnp.dot(left, right, precision=precise, preferred_element_type=jnp.float32)


def lead_dot(left, right):
    return lax.dot_general(
        left, right, (((0,), (0,)), ((), ())), precision=precise, preferred_element_type=jnp.float32
    )


def tail_dot(left, right):
    return lax.dot_general(
        left, right, (((1,), (1,)), ((), ())), precision=precise, preferred_element_type=jnp.float32
    )


def complex_mul(left_re, left_im, right_re, right_im):
    return (
        matmul(left_re, right_re) - matmul(left_im, right_im),
        matmul(left_re, right_im) + matmul(left_im, right_re),
    )


def steering(direction_ids, length):
    element = jnp.arange(length, dtype=jnp.int32)[:, None]
    odd_index = 2 * direction_ids[None, :] + 1
    angle_count = 2 * length
    turns = (element * odd_index - element * angle_count) % (2 * angle_count)
    phase = jnp.pi * turns.astype(jnp.float32) / angle_count
    return (jnp.cos(phase), jnp.sin(phase))


def hermitian_solve(herm_re, herm_im, rhs_re, rhs_im):
    order = herm_re.shape[0]
    embedded = jnp.concatenate(
        [jnp.concatenate([herm_re, -herm_im], 1), jnp.concatenate([herm_im, herm_re], 1)], 0
    )
    factor = jnp.linalg.cholesky(embedded)
    solution = jax.scipy.linalg.cho_solve((factor, True), jnp.concatenate([rhs_re, rhs_im], 0))
    return (solution[:order], solution[order:])


def block_product(current, snap_block):
    inv_re, inv_im = current
    piece_wide = lax.all_gather(snap_block, "row", axis=1, tiled=True).astype(jnp.float32)
    new_re = matmul(inv_re, piece_wide[0]) - matmul(inv_im, piece_wide[1])
    new_im = matmul(inv_re, piece_wide[1]) + matmul(inv_im, piece_wide[0])
    return (new_re, new_im)


def capacitance(snap_block, q_re, q_im):
    snap_wide = snap_block.astype(jnp.float32)
    cap_re = lead_dot(snap_wide[0], q_re) + lead_dot(snap_wide[1], q_im)
    cap_im = lead_dot(snap_wide[0], q_im) - lead_dot(snap_wide[1], q_re)
    return lax.psum((cap_re, cap_im), "row")


def apply_update(current, q_re, q_im, fold_re, fold_im):
    inv_re, inv_im = current
    shard_piece = lax.all_gather(jnp.stack([q_re, q_im]), "row", axis=1, tiled=True)
    new_re = inv_re - tail_dot(fold_re, shard_piece[0]) - tail_dot(fold_im, shard_piece[1])
    new_im = inv_im - tail_dot(fold_im, shard_piece[0]) + tail_dot(fold_re, shard_piece[1])
    updated = jnp.stack([new_re, new_im])
    return (updated[0], updated[1])


def joint_update(current, snap_block):
    q_re, q_im = block_product(current, snap_block)
    cap_re, cap_im = capacitance(snap_block, q_re, q_im)
    half = snap_block.shape[2] // 2
    identity = CYCLE * jnp.eye(half, dtype=jnp.float32)
    rhs_re, rhs_im = (q_re.T, -q_im.T)
    col_count = rhs_re.shape[1]
    first_re, first_im = hermitian_solve(
        identity + cap_re[:half, :half],
        cap_im[:half, :half],
        jnp.concatenate([rhs_re[:half], cap_re[:half, half:]], 1),
        jnp.concatenate([rhs_im[:half], cap_im[:half, half:]], 1),
    )
    base_re, base_im = (first_re[:, :col_count], first_im[:, :col_count])
    cross_re, cross_im = (first_re[:, col_count:], first_im[:, col_count:])
    prod_re, prod_im = complex_mul(cap_re[half:, :half], cap_im[half:, :half], cross_re, cross_im)
    schur_re = identity - cap_re[half:, half:] + prod_re
    schur_im = -cap_im[half:, half:] + prod_im
    lower_re, lower_im = complex_mul(cap_re[half:, :half], cap_im[half:, :half], base_re, base_im)
    second_re, second_im = hermitian_solve(
        schur_re, schur_im, rhs_re[half:] - lower_re, rhs_im[half:] - lower_im
    )
    upper_re, upper_im = complex_mul(cross_re, cross_im, -second_re, -second_im)
    sol_re = jnp.concatenate([base_re - upper_re, -second_re], 0)
    sol_im = jnp.concatenate([base_im - upper_im, -second_im], 0)
    return apply_update(current, q_re, q_im, sol_re.T, -sol_im.T)


def on_device(inverse, cycle, arrivals, departing, directions):
    current = (inverse[0], inverse[1])
    row_count = inverse.shape[1]
    first_row = lax.axis_index("row") * row_count
    weight_list = []
    power_list = []
    for step_index in range(STEPS):
        steer_re, steer_im = steering(directions[step_index], M)
        local_re = lax.dynamic_slice_in_dim(steer_re, first_row, row_count, 0)
        local_im = lax.dynamic_slice_in_dim(steer_im, first_row, row_count, 0)
        app_re, app_im = complex_mul(current[0], current[1], steer_re, steer_im)
        partial_power = jnp.sum(local_re * app_re + local_im * app_im, axis=0)
        power = lax.psum(partial_power, "row")
        departed = jnp.take(cycle, departing[step_index], axis=2)
        current = joint_update(current, jnp.concatenate([arrivals[step_index], departed], axis=2))
        weight_list.append(jnp.stack([M * app_re / power, M * app_im / power]))
        power_list.append(M / power)
    return (jnp.stack([current[0], current[1]]), jnp.stack(weight_list), jnp.stack(power_list))


def solution(mesh):
    in_specs = (
        P("groups", "row", None),
        P("groups", "row", None),
        P("groups", None, "row", None),
        P("groups", None),
        P("groups", None),
    )
    out_specs = (P("groups", "row", None), P("groups", None, "row", None), P("groups", None))
    return jax.shard_map(
        on_device, mesh=mesh, in_specs=in_specs, out_specs=out_specs, check_vma=False
    )
```

profile of v0, /device:TPU:0, one launch (start us, length us, event | category | flops | bytes accessed | tf_op | source)
XLA Modules:
  0.0 946.1 jit_solution(2639609312674014120)
XLA Ops:
  26.9 44.0 %fusion.14 = f32[512,256]{0,1:T(8,128)S(1)} fusion(s32[4096]{0:T(1024)S(1)} %iota_multiply_fusion, s32[512]{0:T(512)S(1)} %bitcast.363, f32[256,4096]{1,0:T(8,128)} %fusion.361), kind=kOutput, calls=%fused_computation.43 | convolution fusion | flops 6473908224 | bytes 4737024 | tf_op jit(solution)/shard_map/dot_general | solution.py:13
  71.0 52.9 %fusion.12 = f32[512,256]{0,1:T(8,128)} fusion(s32[4096]{0:T(1024)S(1)} %iota_multiply_fusion, s32[512]{0:T(512)S(1)} %bitcast.364, f32[256,4096]{1,0:T(8,128)S(1)} %copy-done.11), kind=kOutput, calls=%fused_computation.41 | convolution fusion | flops 6473908224 | bytes 4737024 | tf_op jit(solution)/shard_map/dot_general | solution.py:13
  123.8 52.9 %fusion.71 = f32[256,512]{1,0:T(8,128)} fusion(f32[512,256]{0,1:T(8,128)S(1)} %fusion.14, s32[4096]{0:T(1024)S(1)} %iota_multiply_fusion, s32[512]{0:T(512)S(1)} %bitcast.365, f32[256,4096]{1,0:T(8,128)S(1)} %copy-done.10), kind=kOutput, calls=%fused_computation.85 | convolution fusion | flops 6474039296 | bytes 5261312 | tf_op jit(solution)/shard_map/dot_general | solution.py:13
  176.7 14.3 %fusion.275 = (bf16[1,4096,256]{1,0,2:T(2,128)(2,1)}, bf16[1,4096,256]{1,0,2:T(2,128)(2,1)}) fusion(bf16[2,4096,256]{1,0,2:T(2,128)(2,1)} %all-gather.5.cloned.1.call-done), kind=kLoop, calls=%fused_computation.391 | loop fusion | bytes 8388608 | tf_op jit(solution)/shard_map/slice | solution.py:57
  237.1 68.7 %fusion.11 = (f32[4096,512]{1,0:T(8,128)S(1)}, f32[4096,512]{1,0:T(8,128)S(1)}, f32[4096,512]{1,0:T(8,128)}, f32[4096,512]{1,0:T(8,128)}) fusion(s32[4096]{0:T(1024)S(1)} %iota_multiply_fusion, s32[512]{0:T(512)S(1)} %bitcast.366, s32[512]{0:T(512)S(1)} %bitcast.358), kind=kLoop, calls=%fused_computation.36 | loop fusion | flops 62914560 | bytes 33574912 | tf_op jit(solution)/shard_map/cos | solution.py:41
  305.8 40.4 %add_reduce_fusion.1 = (f32[512]{0:T(512)}, f32[256,512]{1,0:T(8,128)}) fusion(f32[4096,512]{1,0:T(8,128)S(1)} %get-tuple-element.126, s32[]{:T(128)S(6)} %select_n.28, f32[256,512]{1,0:T(8,128)S(1)} %copy-done.19, f32[4096,512]{1,0:T(8,128)S(1)} %get-tuple-element.125, f32[512,256]{0,1:T(8,128)S(1)} %copy-done.28, s32[4096]{0:T(1024)S(1)} %iota_multiply_fusion, ...), kind=kOutput, calls=%fused_computation.143 | convolution fusion | flops 6474563072 | bytes 6836228 | tf_op jit(solution)/shard_map/dot_general | solution.py:13
  379.4 11.7 %cholesky.214 = f32[128,128]{1,0:T(8,128)S(1)} custom-call(f32[128,128]{1,0:T(8,128)S(1)} %cholesky.346), custom_call_target="Cholesky" | custom-call | tf_op jit(solution)/shard_map/jit(cholesky)/cholesky | solution.py:49
  401.5 11.7 %cholesky.231 = f32[128,128]{1,0:T(8,128)S(1)} custom-call(f32[128,128]{1,0:T(8,128)S(1)} %convolution_subtract_fusion.25), custom_call_target="Cholesky" | custom-call | tf_op jit(solution)/shard_map/jit(cholesky)/cholesky | solution.py:49
  420.5 20.1 %custom-call.24 = f32[2,128,128]{1,2,0:T(8,128)S(1)} custom-call(f32[2,128,128]{2,1,0:T(8,128)S(1)} %get-tuple-element.35), custom_call_target="InvertDiagBlocksLowerTriangular" | custom-call | tf_op jit(solution)/shard_map/jit(_cho_solve)/triangular_solve | solution.py:50
  452.6 11.7 %cholesky.248 = f32[128,128]{1,0:T(8,128)S(1)} custom-call(f32[128,128]{1,0:T(8,128)S(1)} %cholesky.349), custom_call_target="Cholesky" | custom-call | tf_op jit(solution)/shard_map/jit(cholesky)/cholesky | solution.py:49
  476.3 11.9 %cholesky.265 = f32[128,128]{1,0:T(8,128)S(1)} custom-call(f32[128,128]{1,0:T(8,128)S(1)} %convolution_subtract_fusion.23), custom_call_target="Cholesky" | custom-call | tf_op jit(solution)/shard_map/jit(cholesky)/cholesky | solution.py:49
  496.8 19.7 %custom-call.26 = f32[2,128,128]{1,2,0:T(8,128)S(1)} custom-call(f32[2,128,128]{2,1,0:T(8,128)S(1)} %get-tuple-element.36), custom_call_target="InvertDiagBlocksLowerTriangular" | custom-call | tf_op jit(solution)/shard_map/jit(_cho_solve)/triangular_solve | solution.py:50
  535.6 39.2 %fusion.30 = f32[256,512]{1,0:T(8,128)} fusion(f32[256,4096]{1,0:T(8,128)S(1)} %convolution_subtract_fusion.4, s32[512]{0:T(512)S(1)} %bitcast.359, s32[4096]{0:T(1024)S(1)} %iota_multiply_fusion), kind=kOutput, calls=%fused_computation.58 | convolution fusion | flops 6473908224 | bytes 4737024 | tf_op jit(solution)/shard_map/dot_general | solution.py:13
  595.2 43.5 %fusion.28 = f32[256,512]{1,0:T(8,128)S(1)} fusion(f32[256,4096]{1,0:T(8,128)} %copy-done.3, s32[512]{0:T(512)S(1)} %bitcast.360, s32[4096]{0:T(1024)S(1)} %iota_multiply_fusion), kind=kOutput, calls=%fused_computation.57 | convolution fusion | flops 6473908224 | bytes 4737024 | tf_op jit(solution)/shard_map/dot_general | solution.py:13
  638.7 38.5 %fusion.60 = f32[256,512]{1,0:T(8,128)S(1)} fusion(f32[256,512]{1,0:T(8,128)S(1)} %copy-done.29, f32[256,4096]{1,0:T(8,128)S(1)} %copy-done.4, s32[512]{0:T(512)S(1)} %bitcast.361, s32[4096]{0:T(1024)S(1)} %iota_multiply_fusion), kind=kOutput, calls=%fused_computation.82 | convolution fusion | flops 6474039296 | bytes 5261312 | tf_op jit(solution)/shard_map/dot_general | solution.py:13
  677.2 53.5 %add_reduce_fusion = (f32[512]{0:T(512)S(1)}, f32[256,512]{1,0:T(8,128)S(1)}) fusion(f32[4096,512]{1,0:T(8,128)} %get-tuple-element.129, s32[]{:T(128)S(6)} %select_n.28, f32[256,512]{1,0:T(8,128)S(1)} %fusion.60, f32[4096,512]{1,0:T(8,128)} %get-tuple-element.130, f32[256,512]{1,0:T(8,128)S(1)} %fusion.28, f32[256,4096]{1,0:T(8,128)S(1)} %copy-done.2, ...), kind=kOutput, calls=%fused_computation.140 | convolution fusion | flops 6474563072 | bytes 6836228 | tf_op jit(solution)/shard_map/dot_general | solution.py:13
  730.7 36.4 %all-reduce.1 = (f32[512]{0:T(512)S(1)}, f32[512]{0:T(512)S(1)}) all-reduce(f32[512]{0:T(512)S(1)} %get-tuple-element.157, f32[512]{0:T(512)S(1)} %copy-done.25), channel_id=1, replica_groups=mesh['groups'=2,'row'=16] {'row'}, use_global_device_ids=true, to_apply=%region_11.16 | all-reduce | flops 1024 | bytes 8192 | tf_op jit(solution)/shard_map/psum | solution.py:118
  771.8 11.7 %cholesky.282 = f32[128,128]{1,0:T(8,128)S(1)} custom-call(f32[128,128]{1,0:T(8,128)S(1)} %cholesky.352), custom_call_target="Cholesky" | custom-call | tf_op jit(solution)/shard_map/jit(cholesky)/cholesky | solution.py:49
  793.9 11.7 %cholesky.299 = f32[128,128]{1,0:T(8,128)S(1)} custom-call(f32[128,128]{1,0:T(8,128)S(1)} %convolution_subtract_fusion.22), custom_call_target="Cholesky" | custom-call | tf_op jit(solution)/shard_map/jit(cholesky)/cholesky | solution.py:49
  812.5 19.8 %custom-call.28 = f32[2,128,128]{1,2,0:T(8,128)S(1)} custom-call(f32[2,128,128]{2,1,0:T(8,128)S(1)} %get-tuple-element.37), custom_call_target="InvertDiagBlocksLowerTriangular" | custom-call | tf_op jit(solution)/shard_map/jit(_cho_solve)/triangular_solve | solution.py:50
  837.0 11.7 %cholesky.316 = f32[128,128]{1,0:T(8,128)S(1)} custom-call(f32[128,128]{1,0:T(8,128)S(1)} %cholesky.355), custom_call_target="Cholesky" | custom-call | tf_op jit(solution)/shard_map/jit(cholesky)/cholesky | solution.py:49
  859.0 11.9 %cholesky.333 = f32[128,128]{1,0:T(8,128)S(1)} custom-call(f32[128,128]{1,0:T(8,128)S(1)} %convolution_subtract_fusion.20), custom_call_target="Cholesky" | custom-call | tf_op jit(solution)/shard_map/jit(cholesky)/cholesky | solution.py:49
  877.8 19.7 %custom-call.30 = f32[2,128,128]{1,2,0:T(8,128)S(1)} custom-call(f32[2,128,128]{2,1,0:T(8,128)S(1)} %get-tuple-element.38), custom_call_target="InvertDiagBlocksLowerTriangular" | custom-call | tf_op jit(solution)/shard_map/jit(_cho_solve)/triangular_solve | solution.py:50
  902.1 12.5 %convolution_subtract_fusion.2 = f32[256,4096]{1,0:T(8,128)S(1)} fusion(f32[256,4096]{1,0:T(8,128)} %copy-done.1, f32[2,4096,256]{2,1,0:T(8,128)} %all-gather.11.cloned.1.call-done, f32[128,256]{1,0:T(8,128)S(1)} %convolution_negate_fusion, f32[128,256]{1,0:T(8,128)S(1)} %fusion.108), kind=kOutput, calls=%fused_computation.28 | convolution fusion | flops 3222339584 | bytes 12845056 | tf_op jit(solution)/shard_map/dot_general | solution.py:23
  (297 shorter events, 272.0 us)
Async XLA Ops:
  7.2 169.6 %all-gather.5.cloned.1.call-start = ((), (), s32[]{:S(2)}) async-start(), calls=%async_computation | async-start | bytes 4456448 | tf_op jit(solution)/shard_map/all_gather | solution.py:56
  13.8 333.1 %all-gather.9.cloned.1.call-start = ((), (), s32[]{:S(2)}) async-start(), calls=%async_computation.2 | async-start | bytes 4456448 | tf_op jit(solution)/shard_map/all_gather | solution.py:56
  16.2 361.3 %all-reduce.9.cloned.1.call-start = ((), (), s32[]{:S(2)}) async-start(), calls=%async_computation.5 | async-start | bytes 1048576 | tf_op jit(solution)/shard_map/psum | solution.py:66
  26.9 210.2 %copy-start.22 = (s32[1,512]{1,0:T(1,128)}, s32[1,512]{1,0:T(1,128)S(1)}, u32[]{:S(2)}) copy-start(s32[1,512]{1,0:T(1,128)S(1)} %get-tuple-element.132) | copy-start | bytes 6148
  26.9 44.0 %copy-start.11 = (f32[256,4096]{1,0:T(8,128)S(1)}, f32[256,4096]{1,0:T(8,128)}, u32[]{:S(2)}) copy-start(f32[256,4096]{1,0:T(8,128)} %fusion.359) | copy-start | bytes 12582916
  70.9 52.9 %copy-start.10 = (f32[256,4096]{1,0:T(8,128)S(1)}, f32[256,4096]{1,0:T(8,128)}, u32[]{:S(2)}) copy-start(f32[256,4096]{1,0:T(8,128)} %fusion.363) | copy-start | bytes 12582916
  232.1 291.9 %all-gather.7.cloned.1.call-start = ((), (), s32[]{:S(2)}) async-start(), calls=%async_computation.1 | async-start | bytes 8912896 | tf_op jit(solution)/shard_map/all_gather | solution.py:71
  234.5 535.2 %all-reduce.7.cloned.1.call-start = ((), (), s32[]{:S(2)}) async-start(), calls=%async_computation.4 | async-start | bytes 1048576 | tf_op jit(solution)/shard_map/psum | solution.py:66
  237.1 68.7 %copy-start.19 = (f32[256,512]{1,0:T(8,128)S(1)}, f32[256,512]{1,0:T(8,128)}, u32[]{:S(2)}) copy-start(f32[256,512]{1,0:T(8,128)} %fusion.71) | copy-start | bytes 1572868
  237.1 68.7 %copy-start.28 = (f32[512,256]{0,1:T(8,128)S(1)}, f32[512,256]{0,1:T(8,128)}, u32[]{:S(2)}) copy-start(f32[512,256]{0,1:T(8,128)} %fusion.12) | copy-start | bytes 1572868
  531.7 45.2 %slice-start.2 = ((s8[8388608]{0:T(1024)(128)(4,1)}), s8[4194304]{0:T(1024)(128)(4,1)S(1)}, s32[]{:S(2)}) async-start(s8[8388608]{0:T(1024)(128)(4,1)} %bitcast.346), calls=%async_computation.8 | async-start | bytes 8388608
  535.6 53.5 %copy-start.1 = (f32[256,4096]{1,0:T(8,128)}, f32[256,4096]{1,0:T(8,128)S(1)}, u32[]{:S(2)}) copy-start(f32[256,4096]{1,0:T(8,128)S(1)} %convolution_subtract_fusion.4) | copy-start | bytes 12582916
  535.6 41.3 %slice-start.3 = ((s8[8388608]{0:T(1024)(128)(4,1)}), s8[4194304]{0:T(1024)(128)(4,1)S(1)}, s32[]{:S(2)}) async-start(s8[8388608]{0:T(1024)(128)(4,1)} %bitcast.346), calls=%async_computation.9 | async-start | bytes 8388608
  594.1 308.0 %all-gather.11.cloned.1.call-start = ((), (), s32[]{:S(2)}) async-start(), calls=%async_computation.3 | async-start | bytes 8912896 | tf_op jit(solution)/shard_map/all_gather | solution.py:71
  594.2 44.5 %copy-start.14 = (f32[256,256]{0,1:T(8,128)}, f32[256,256]{0,1:T(8,128)S(1)}, u32[]{:S(2)}) copy-start(f32[256,256]{0,1:T(8,128)S(1)} %negate_bitcast_fusion) | copy-start | bytes 786436
  595.2 43.5 %copy-start.4 = (f32[256,4096]{1,0:T(8,128)S(1)}, f32[256,4096]{1,0:T(8,128)}, u32[]{:S(2)}) copy-start(f32[256,4096]{1,0:T(8,128)} %copy-done.3) | copy-start | bytes 12582916
  595.2 43.5 %copy-start.29 = (f32[256,512]{1,0:T(8,128)S(1)}, f32[256,512]{1,0:T(8,128)}, u32[]{:S(2)}) copy-start(f32[256,512]{1,0:T(8,128)} %fusion.30) | copy-start | bytes 1572868
  677.2 53.5 %copy-start.25 = (f32[512]{0:T(512)S(1)}, f32[512]{0:T(512)}, u32[]{:S(2)}) copy-start(f32[512]{0:T(512)} %get-tuple-element.159) | copy-start | bytes 6148
  677.2 90.5 %copy-start.20 = (f32[256,512]{1,0:T(8,128)S(1)}, f32[256,512]{1,0:T(8,128)}, u32[]{:S(2)}) copy-start(f32[256,512]{1,0:T(8,128)} %fusion.71) | copy-start | bytes 1572868
  677.2 90.5 %copy-start.21 = (f32[256,512]{1,0:T(8,128)S(1)}, f32[256,512]{1,0:T(8,128)}, u32[]{:S(2)}) copy-start(f32[256,512]{1,0:T(8,128)} %get-tuple-element.160) | copy-start | bytes 1572868
  767.9 64.9 %slice-start.4 = ((f32[256,256]{0,1:T(8,128)}), f32[128,256]{0,1:T(8,128)S(1)}, s32[]{:S(2)}) async-start(f32[256,256]{0,1:T(8,128)} %copy-done.14), calls=%async_computation.10 | async-start | bytes 262144 | tf_op jit(solution)/shard_map/slice | solution.py:89
  769.7 129.3 %copy-start.15 = (f32[256,256]{0,1:T(8,128)S(1)}, f32[256,256]{0,1:T(8,128)}, u32[]{:S(2)}) copy-start(f32[256,256]{0,1:T(8,128)} %copy-done.14) | copy-start | bytes 786436
  769.7 66.1 %copy-start.16 = (f32[256,256]{0,1:T(8,128)S(1)}, f32[256,256]{0,1:T(8,128)}, u32[]{:S(2)}) copy-start(f32[256,256]{0,1:T(8,128)} %get-tuple-element.73) | copy-start | bytes 786436
  769.7 66.4 %copy-start.18 = (f32[256,256]{0,1:T(8,128)S(1)}, f32[256,256]{0,1:T(8,128)}, u32[]{:S(2)}) copy-start(f32[256,256]{0,1:T(8,128)} %get-tuple-element.74) | copy-start | bytes 786436
  (17 other events, 243.9 us)
Sparse Core Ops, SparseCore 0:
  13.9 67.0 all-gather.4
  83.1 62.5 all-gather.8
  232.3 93.4 all-reduce.8
  327.7 78.2 all-gather.6
  594.3 93.5 all-reduce.6
  689.9 75.3 all-gather.10
where the time goes:
time: 954 us; the launch traced here: 946 us
  matrix products  478 us (50%)
  other arithmetic  306 us (32%)
  local copies, waits for them, and re-layouts  104 us (11%)
  blocking collectives  36.4 us (4%)
  between operations  21 us (2%)
    dot_general x40, matrix products, matmul(): jnp.dot(left, right, precision=precise, preferred_element_type=jnp.float32)  408 us
    another operation x28, other arithmetic, hermitian_solve(): factor = jnp.linalg.cholesky(embedded)  139 us
    another operation x9, other arithmetic, hermitian_solve(): jax.scipy.linalg.cho_solve((factor, True), jnp.concatenate([rhs_re, rhs_i...  80.9 us
    cos x1, other arithmetic, steering(): return (jnp.cos(phase), jnp.sin(phase))  68.7 us
    slice x6, local copies, waits for them, and re-layouts, block_product(): new_re = matmul(inv_re, piece_wide[0]) - matmul(inv_im, piece_wide[1])  63.9 us
    dot_general x8, matrix products, tail_dot(): lax.dot_general(left, right, (((1,), (1,)), ((), ())), precision=precise,...  52.1 us
    psum x1, blocking collectives, on_device(): power = lax.psum(partial_power, 'row')  36.4 us
  transfers between devices with their start and end apart: 6, of which 0 were waited for; matrix products, arithmetic and copies ran while one was open for 82% of the time, Pallas kernels for 0%

commit v1 on v0

--- a/solution.py
+++ b/solution.py
@@ -115,7 +115,7 @@
         local_im = lax.dynamic_slice_in_dim(steer_im, first_row, row_count, 0)
         app_re, app_im = complex_mul(current[0], current[1], steer_re, steer_im)
         partial_power = jnp.sum(local_re * app_re + local_im * app_im, axis=0)
-        power = lax.psum(partial_power, "row")
+        power = jnp.sum(lax.all_gather(partial_power, "row"), axis=0)
         departed = jnp.take(cycle, departing[step_index], axis=2)
         current = joint_update(current, jnp.concatenate([arrivals[step_index], departed], axis=2))
         weight_list.append(jnp.stack([M * app_re / power, M * app_im / power]))

time: 954 us -> 1000 us (1.048)
  matrix products: 478 us -> 499 us
  other arithmetic: 306 us -> 317 us
  local copies, waits for them, and re-layouts: 104 us -> 115 us
    all_gather x0 -> x2, blocking collectives: none -> 41.3 us  [on_device(): power = jnp.sum(lax.all_gather(partial_power, 'row'), axis=0)]
    psum x1 -> x0, blocking collectives: 36.4 us -> none  [on_device(): power = lax.psum(partial_power, 'row')]
    dot_general x40, matrix products: 408 us -> 420 us  [matmul(): jnp.dot(left, right, precision=precise, preferred_element_type=jnp.float32)]
  transfers between devices with their start and end apart: 6 -> 6, of which waited for: 0 -> 0; matrix products, arithmetic and copies ran while one was open for 82% -> 86% of each run, Pallas kernels for 0% -> 0%
where the time goes in v1:
time: 1000 us; the launch traced here: 994 us
  matrix products  499 us (50%)
  other arithmetic  317 us (32%)
  local copies, waits for them, and re-layouts  115 us (12%)
  blocking collectives  41.3 us (4%)
  between operations  20.9 us (2%)
    dot_general x40, matrix products, matmul(): jnp.dot(left, right, precision=precise, preferred_element_type=jnp.float32)  420 us
    another operation x28, other arithmetic, hermitian_solve(): factor = jnp.linalg.cholesky(embedded)  146 us
    another operation x9, other arithmetic, hermitian_solve(): jax.scipy.linalg.cho_solve((factor, True), jnp.concatenate([rhs_re, rhs_i...  82.3 us
    cos x1, other arithmetic, steering(): return (jnp.cos(phase), jnp.sin(phase))  68.7 us
    slice x6, local copies, waits for them, and re-layouts, block_product(): new_re = matmul(inv_re, piece_wide[0]) - matmul(inv_im, piece_wide[1])  64.1 us
    dot_general x8, matrix products, tail_dot(): lax.dot_general(left, right, (((1,), (1,)), ((), ())), precision=precise,...  51.8 us
    all_gather x2, blocking collectives, on_device(): power = jnp.sum(lax.all_gather(partial_power, 'row'), axis=0)  41.3 us
  transfers between devices with their start and end apart: 6, of which 0 were waited for; matrix products, arithmetic and copies ran while one was open for 86% of the time, Pallas kernels for 0%

profile of v1, /device:TPU:0, one launch (start us, length us, event | category | flops | bytes accessed | tf_op | source)
XLA Modules:
  0.0 993.7 jit_solution(4882424606158126414)
XLA Ops:
  26.9 44.0 %fusion.14 = f32[512,256]{0,1:T(8,128)S(1)} fusion(s32[4096]{0:T(1024)S(1)} %iota_multiply_fusion, s32[512]{0:T(512)S(1)} %bitcast.365, f32[256,4096]{1,0:T(8,128)} %fusion.361), kind=kOutput, calls=%fused_computation.43 | convolution fusion | flops 6473908224 | bytes 4737024 | tf_op jit(solution)/shard_map/dot_general | solution.py:13
  70.9 52.9 %fusion.12 = f32[512,256]{0,1:T(8,128)} fusion(s32[4096]{0:T(1024)S(1)} %iota_multiply_fusion, s32[512]{0:T(512)S(1)} %bitcast.366, f32[256,4096]{1,0:T(8,128)S(1)} %copy-done.12), kind=kOutput, calls=%fused_computation.41 | convolution fusion | flops 6473908224 | bytes 4737024 | tf_op jit(solution)/shard_map/dot_general | solution.py:13
  123.8 52.9 %fusion.71 = f32[256,512]{1,0:T(8,128)} fusion(f32[512,256]{0,1:T(8,128)S(1)} %fusion.14, s32[4096]{0:T(1024)S(1)} %iota_multiply_fusion, s32[512]{0:T(512)S(1)} %bitcast.367, f32[256,4096]{1,0:T(8,128)S(1)} %copy-done.11), kind=kOutput, calls=%fused_computation.85 | convolution fusion | flops 6474039296 | bytes 5261312 | tf_op jit(solution)/shard_map/dot_general | solution.py:13
  176.7 14.5 %fusion.275 = (bf16[1,4096,256]{1,0,2:T(2,128)(2,1)}, bf16[1,4096,256]{1,0,2:T(2,128)(2,1)}) fusion(bf16[2,4096,256]{1,0,2:T(2,128)(2,1)} %all-gather.9.cloned.1.call-done), kind=kLoop, calls=%fused_computation.391 | loop fusion | bytes 8388608 | tf_op jit(solution)/shard_map/slice | solution.py:57
  239.5 68.7 %fusion.11 = (f32[4096,512]{1,0:T(8,128)S(1)}, f32[4096,512]{1,0:T(8,128)S(1)}, f32[4096,512]{1,0:T(8,128)}, f32[4096,512]{1,0:T(8,128)}) fusion(s32[4096]{0:T(1024)S(1)} %iota_multiply_fusion, s32[512]{0:T(512)S(1)} %bitcast.368, s32[512]{0:T(512)S(1)} %bitcast.360), kind=kLoop, calls=%fused_computation.36 | loop fusion | flops 62914560 | bytes 33574912 | tf_op jit(solution)/shard_map/cos | solution.py:41
  308.2 39.4 %add_reduce_fusion.1 = (f32[512]{0:T(512)S(1)}, f32[256,512]{1,0:T(8,128)S(1)}) fusion(f32[4096,512]{1,0:T(8,128)S(1)} %get-tuple-element.124, s32[]{:T(128)S(6)} %select_n.28, f32[256,512]{1,0:T(8,128)S(1)} %copy-done.30, f32[4096,512]{1,0:T(8,128)S(1)} %get-tuple-element.123, f32[512,256]{0,1:T(8,128)S(1)} %copy-done.38, ...), kind=kOutput, calls=%fused_computation.143 | convolution fusion | flops 6474563072 | bytes 6836228 | tf_op jit(solution)/shard_map/dot_general | solution.py:13
  347.7 23.7 %all-gather.2 = f32[16,1,512]{2,1,0:T(1,128)S(1)} all-gather(f32[1,1,512]{2,1,0:T(1,128)S(1)} %bitcast.373), channel_id=2, replica_groups=mesh['groups'=2,'row'=16] {'row'}, dimensions={0}, use_global_device_ids=true | all-gather | bytes 34816 | tf_op jit(solution)/shard_map/all_gather | solution.py:118
  433.1 11.7 %cholesky.231 = f32[128,128]{1,0:T(8,128)S(1)} custom-call(f32[128,128]{1,0:T(8,128)S(1)} %convolution_subtract_fusion.25), custom_call_target="Cholesky" | custom-call | tf_op jit(solution)/shard_map/jit(cholesky)/cholesky | solution.py:49
  452.9 20.1 %custom-call.24 = f32[2,128,128]{1,2,0:T(8,128)S(1)} custom-call(f32[2,128,128]{2,1,0:T(8,128)S(1)} %get-tuple-element.35), custom_call_target="InvertDiagBlocksLowerTriangular" | custom-call | tf_op jit(solution)/shard_map/jit(_cho_solve)/triangular_solve | solution.py:50
  489.9 12.3 %cholesky.248 = f32[128,128]{1,0:T(8,128)} custom-call(f32[128,128]{1,0:T(8,128)S(1)} %cholesky.349), custom_call_target="Cholesky" | custom-call | tf_op jit(solution)/shard_map/jit(cholesky)/cholesky | solution.py:49
  519.2 13.3 %cholesky.265 = f32[128,128]{1,0:T(8,128)} custom-call(f32[128,128]{1,0:T(8,128)} %convolution_subtract_fusion.23), custom_call_target="Cholesky" | custom-call | tf_op jit(solution)/shard_map/jit(cholesky)/cholesky | solution.py:49
  544.8 21.1 %custom-call.26 = f32[2,128,128]{1,2,0:T(8,128)} custom-call(f32[2,128,128]{2,1,0:T(8,128)} %get-tuple-element.36), custom_call_target="InvertDiagBlocksLowerTriangular" | custom-call | tf_op jit(solution)/shard_map/jit(_cho_solve)/triangular_solve | solution.py:50
  610.2 43.5 %fusion.30 = f32[256,512]{1,0:T(8,128)S(1)} fusion(f32[256,4096]{1,0:T(8,128)} %copy-done.1, s32[512]{0:T(512)S(1)} %bitcast.361, s32[4096]{0:T(1024)S(1)} %iota_multiply_fusion), kind=kOutput, calls=%fused_computation.58 | convolution fusion | flops 6473908224 | bytes 4737024 | tf_op jit(solution)/shard_map/dot_general | solution.py:13
  653.8 52.0 %fusion.28 = f32[256,512]{1,0:T(8,128)S(1)} fusion(f32[256,4096]{1,0:T(8,128)S(1)} %copy-done.4, s32[512]{0:T(512)S(1)} %bitcast.362, s32[4096]{0:T(1024)S(1)} %iota_multiply_fusion), kind=kOutput, calls=%fused_computation.57 | convolution fusion | flops 6473908224 | bytes 4737024 | tf_op jit(solution)/shard_map/dot_general | solution.py:13
  705.8 38.3 %fusion.60 = f32[256,512]{1,0:T(8,128)S(1)} fusion(f32[256,512]{1,0:T(8,128)S(1)} %fusion.30, f32[256,4096]{1,0:T(8,128)S(1)} %copy-done.4, s32[512]{0:T(512)S(1)} %bitcast.363, s32[4096]{0:T(1024)S(1)} %iota_multiply_fusion), kind=kOutput, calls=%fused_computation.82 | convolution fusion | flops 6474039296 | bytes 5261312 | tf_op jit(solution)/shard_map/dot_general | solution.py:13
  744.2 53.5 %add_reduce_fusion = (f32[512]{0:T(512)S(1)}, f32[256,512]{1,0:T(8,128)S(1)}) fusion(f32[4096,512]{1,0:T(8,128)} %get-tuple-element.127, s32[]{:T(128)S(6)} %select_n.28, f32[256,512]{1,0:T(8,128)S(1)} %fusion.60, f32[4096,512]{1,0:T(8,128)} %get-tuple-element.128, f32[256,512]{1,0:T(8,128)S(1)} %fusion.28, f32[256,4096]{1,0:T(8,128)S(1)} %copy-done.2, ...), kind=kOutput, calls=%fused_computation.140 | convolution fusion | flops 6474563072 | bytes 6836228 | tf_op jit(solution)/shard_map/dot_general | solution.py:13
  797.7 17.7 %all-gather.3 = f32[16,1,512]{2,1,0:T(1,128)S(1)} all-gather(f32[1,1,512]{2,1,0:T(1,128)S(1)} %bitcast.372), channel_id=3, replica_groups=mesh['groups'=2,'row'=16] {'row'}, dimensions={0}, use_global_device_ids=true | all-gather | bytes 34816 | tf_op jit(solution)/shard_map/all_gather | solution.py:118
  819.9 11.7 %cholesky.282 = f32[128,128]{1,0:T(8,128)S(1)} custom-call(f32[128,128]{1,0:T(8,128)S(1)} %cholesky.352), custom_call_target="Cholesky" | custom-call | tf_op jit(solution)/shard_map/jit(cholesky)/cholesky | solution.py:49
  842.0 11.7 %cholesky.299 = f32[128,128]{1,0:T(8,128)S(1)} custom-call(f32[128,128]{1,0:T(8,128)S(1)} %convolution_subtract_fusion.22), custom_call_target="Cholesky" | custom-call | tf_op jit(solution)/shard_map/jit(cholesky)/cholesky | solution.py:49
  860.3 19.8 %custom-call.28 = f32[2,128,128]{1,2,0:T(8,128)S(1)} custom-call(f32[2,128,128]{2,1,0:T(8,128)S(1)} %get-tuple-element.37), custom_call_target="InvertDiagBlocksLowerTriangular" | custom-call | tf_op jit(solution)/shard_map/jit(_cho_solve)/triangular_solve | solution.py:50
  884.8 11.7 %cholesky.316 = f32[128,128]{1,0:T(8,128)S(1)} custom-call(f32[128,128]{1,0:T(8,128)S(1)} %cholesky.355), custom_call_target="Cholesky" | custom-call | tf_op jit(solution)/shard_map/jit(cholesky)/cholesky | solution.py:49
  906.9 11.9 %cholesky.333 = f32[128,128]{1,0:T(8,128)S(1)} custom-call(f32[128,128]{1,0:T(8,128)S(1)} %convolution_subtract_fusion.20), custom_call_target="Cholesky" | custom-call | tf_op jit(solution)/shard_map/jit(cholesky)/cholesky | solution.py:49
  925.4 19.7 %custom-call.30 = f32[2,128,128]{1,2,0:T(8,128)S(1)} custom-call(f32[2,128,128]{2,1,0:T(8,128)S(1)} %get-tuple-element.38), custom_call_target="InvertDiagBlocksLowerTriangular" | custom-call | tf_op jit(solution)/shard_map/jit(_cho_solve)/triangular_solve | solution.py:50
  949.7 12.5 %convolution_subtract_fusion.2 = f32[256,4096]{1,0:T(8,128)S(1)} fusion(f32[256,4096]{1,0:T(8,128)} %copy-done.1, f32[2,4096,256]{2,1,0:T(8,128)} %all-gather.15.cloned.1.call-done, f32[128,256]{1,0:T(8,128)S(1)} %convolution_negate_fusion, f32[128,256]{1,0:T(8,128)S(1)} %fusion.108), kind=kOutput, calls=%fused_computation.28 | convolution fusion | flops 3222339584 | bytes 12845056 | tf_op jit(solution)/shard_map/dot_general | solution.py:23
  (318 shorter events, 312.7 us)
Async XLA Ops:
  7.2 169.6 %all-gather.9.cloned.1.call-start = ((), (), s32[]{:S(2)}) async-start(), calls=%async_computation | async-start | bytes 4456448 | tf_op jit(solution)/shard_map/all_gather | solution.py:56
  13.8 360.9 %all-gather.13.cloned.1.call-start = ((), (), s32[]{:S(2)}) async-start(), calls=%async_computation.2 | async-start | bytes 4456448 | tf_op jit(solution)/shard_map/all_gather | solution.py:56
  16.2 389.2 %all-reduce.8.cloned.1.call-start = ((), (), s32[]{:S(2)}) async-start(), calls=%async_computation.5 | async-start | bytes 1048576 | tf_op jit(solution)/shard_map/psum | solution.py:66
  26.9 212.6 %copy-start.32 = (s32[1,512]{1,0:T(1,128)}, s32[1,512]{1,0:T(1,128)S(1)}, u32[]{:S(2)}) copy-start(s32[1,512]{1,0:T(1,128)S(1)} %get-tuple-element.130) | copy-start | bytes 6148
  26.9 44.0 %copy-start.12 = (f32[256,4096]{1,0:T(8,128)S(1)}, f32[256,4096]{1,0:T(8,128)}, u32[]{:S(2)}) copy-start(f32[256,4096]{1,0:T(8,128)} %fusion.359) | copy-start | bytes 12582916
  70.9 52.9 %copy-start.11 = (f32[256,4096]{1,0:T(8,128)S(1)}, f32[256,4096]{1,0:T(8,128)}, u32[]{:S(2)}) copy-start(f32[256,4096]{1,0:T(8,128)} %fusion.363) | copy-start | bytes 12582916
  210.2 16.1 %slice-start = ((s8[8388608]{0:T(1024)(128)(4,1)}), s8[4194304]{0:T(1024)(128)(4,1)S(1)}, s32[]{:S(2)}) async-start(s8[8388608]{0:T(1024)(128)(4,1)} %bitcast.346), calls=%async_computation.6 | async-start | bytes 8388608
  221.0 153.1 %copy-start.18 = (f32[256,256]{1,0:T(8,128)}, f32[256,256]{1,0:T(8,128)S(1)}, u32[]{:S(2)}) copy-start(f32[256,256]{1,0:T(8,128)S(1)} %get-tuple-element.139) | copy-start | bytes 786436
  231.6 346.6 %all-gather.11.cloned.1.call-start = ((), (), s32[]{:S(2)}) async-start(), calls=%async_computation.1 | async-start | bytes 8912896 | tf_op jit(solution)/shard_map/all_gather | solution.py:71
  237.1 580.7 %all-reduce.6.cloned.1.call-start = ((), (), s32[]{:S(2)}) async-start(), calls=%async_computation.4 | async-start | bytes 1048576 | tf_op jit(solution)/shard_map/psum | solution.py:66
  239.5 68.7 %copy-start.10 = (f32[256,4096]{1,0:T(8,128)S(1)}, f32[256,4096]{1,0:T(8,128)}, u32[]{:S(2)}) copy-start(f32[256,4096]{1,0:T(8,128)} %fusion.84.clone.5) | copy-start | bytes 12582916
  239.5 68.7 %copy-start.30 = (f32[256,512]{1,0:T(8,128)S(1)}, f32[256,512]{1,0:T(8,128)}, u32[]{:S(2)}) copy-start(f32[256,512]{1,0:T(8,128)} %fusion.71) | copy-start | bytes 1572868
  239.5 68.7 %copy-start.38 = (f32[512,256]{0,1:T(8,128)S(1)}, f32[512,256]{0,1:T(8,128)}, u32[]{:S(2)}) copy-start(f32[512,256]{0,1:T(8,128)} %fusion.12) | copy-start | bytes 1572868
  589.4 14.6 %copy-start.1 = (f32[256,4096]{1,0:T(8,128)}, f32[256,4096]{1,0:T(8,128)S(1)}, u32[]{:S(2)}) copy-start(f32[256,4096]{1,0:T(8,128)S(1)} %convolution_subtract_fusion.4) | copy-start | bytes 12582916
  609.2 340.5 %all-gather.15.cloned.1.call-start = ((), (), s32[]{:S(2)}) async-start(), calls=%async_computation.3 | async-start | bytes 8912896 | tf_op jit(solution)/shard_map/all_gather | solution.py:71
  610.2 43.5 %copy-start.4 = (f32[256,4096]{1,0:T(8,128)S(1)}, f32[256,4096]{1,0:T(8,128)}, u32[]{:S(2)}) copy-start(f32[256,4096]{1,0:T(8,128)} %copy-done.3) | copy-start | bytes 12582916
  653.8 52.1 %copy-start.20 = (f32[256,256]{0,1:T(8,128)}, f32[256,256]{0,1:T(8,128)S(1)}, u32[]{:S(2)}) copy-start(f32[256,256]{0,1:T(8,128)S(1)} %negate_bitcast_fusion) | copy-start | bytes 786436
  705.8 38.3 %copy-start.2 = (f32[256,4096]{1,0:T(8,128)S(1)}, f32[256,4096]{1,0:T(8,128)}, u32[]{:S(2)}) copy-start(f32[256,4096]{1,0:T(8,128)} %copy-done.1) | copy-start | bytes 12582916
  744.2 71.2 %copy-start.34 = (f32[512]{0:T(512)S(1)}, f32[512]{0:T(512)}, u32[]{:S(2)}) copy-start(f32[512]{0:T(512)} %broadcast_divide_fusion.1) | copy-start | bytes 6148
  797.7 58.6 %copy-start.37 = (s32[2,2]{1,0:T(2,128)S(1)}, s32[2,2]{1,0:T(2,128)}, u32[]{:S(2)}) copy-start(s32[2,2]{1,0:T(2,128)} %get-tuple-element.379) | copy-start | bytes 52
  797.7 82.9 %slice-start.4 = ((f32[256,256]{0,1:T(8,128)}), f32[128,256]{0,1:T(8,128)S(1)}, s32[]{:S(2)}) async-start(f32[256,256]{0,1:T(8,128)} %copy-done.20), calls=%async_computation.10 | async-start | bytes 262144 | tf_op jit(solution)/shard_map/slice | solution.py:89
  817.8 128.8 %copy-start.21 = (f32[256,256]{0,1:T(8,128)S(1)}, f32[256,256]{0,1:T(8,128)}, u32[]{:S(2)}) copy-start(f32[256,256]{0,1:T(8,128)} %copy-done.20) | copy-start | bytes 786436
  817.8 65.8 %copy-start.22 = (f32[256,256]{0,1:T(8,128)S(1)}, f32[256,256]{0,1:T(8,128)}, u32[]{:S(2)}) copy-start(f32[256,256]{0,1:T(8,128)} %get-tuple-element.71) | copy-start | bytes 786436
  817.8 66.2 %copy-start.25 = (f32[256,256]{0,1:T(8,128)S(1)}, f32[256,256]{0,1:T(8,128)}, u32[]{:S(2)}) copy-start(f32[256,256]{0,1:T(8,128)} %get-tuple-element.72) | copy-start | bytes 786436
  (26 other events, 140.2 us)
Sparse Core Ops, SparseCore 0:
  13.9 67.0 all-gather.8
  83.1 62.5 all-gather.12
  231.7 93.4 all-reduce.7
  327.1 78.2 all-gather.10
  609.3 88.1 all-reduce.5
  699.6 74.8 all-gather.14
